TPU v7x, 256 devices: a whole 4x4x8 slice. The times are simulated.
256 devices in a mesh: segment: 4 (over y), seq: 64 (over x, z, core).
Axes of the slice: x: 4, y: 4, z: 8, core: 2. Of those that a mesh axis runs over, the one named last changes fastest.
Arguments:
- held: bfloat16 [4, 8192, 1024], P('segment', 'seq'), may hold values from -6 to 6
- log_decay: float32 [4, 8192, 8], P('segment', 'seq'), may hold values from -2 to 0, as said below
- route_ids: int32 [4, 64, 1], P('segment'), may hold values from 0 to 7; in each aligned block of 8 rows (0 to 7, 8 to 15, ..., all dimensions but the last counted through in order) at most 2 rows name the same one
- norm_gain: float32 [4, 1024], P('segment'), may hold values from 0.1 to 1.9
- qkv_weight: bfloat16 [4, 1024, 3072], P('segment'), may hold values from -0.1875 to 0.1875
- beta_weight: bfloat16 [4, 1024, 8], P('segment'), may hold values from -0.1875 to 0.1875
- out_gain: float32 [4, 128], P('segment'), may hold values from 0.1 to 1.9
- out_weight: bfloat16 [4, 1024, 1024], P('segment'), may hold values from -0.1875 to 0.1875
- ffn_gain: float32 [4, 1024], P('segment'), may hold values from 0.1 to 1.9
- gate_weight: bfloat16 [4, 64, 1024, 512], P('segment', 'seq'), may hold values from -0.1875 to 0.1875
- up_weight: bfloat16 [4, 64, 1024, 512], P('segment', 'seq'), may hold values from -0.1875 to 0.1875
- down_weight: bfloat16 [4, 64, 512, 1024], P('segment', 'seq'), may hold values from -0.09375 to 0.09375
Outputs:
- next_held: bfloat16 [4, 8192, 1024], P('segment', 'seq')
Inputs may be any that keep to these rules, and one draw needn't show every extreme that they name: `log_decay`: every entry is negative. `route_ids`: within each aligned group of 8 consecutive blocks of a section no machine type is named more than 2 times, and in some group of every draw one type is named exactly 2 times.
All inputs are finite; a program needn't handle non-finite values.
Results may differ from a plain program's by a relative error of at most 0.018.
Values may be sent and summed in bfloat16 or wider, within the bound.
A program may use at most 192 MiB of HBM per device.

v0:
```python
from functools import partial

import jax
import jax.numpy as jnp
from jax import lax
from jax.sharding import PartitionSpec as P

EXPERTS = 8
BLOCK = 128


def swapped(block, axis, distance):
    count = lax.axis_size(axis)
    route = []
    for low in range(count):
        high = low | 1 << distance
        if high != low and high < count:
            route += [(low, high), (high, low)]
    return lax.ppermute(block, axis, route)


def carried_in(shard, axis, join, neutral):
    place = lax.axis_index(axis)
    gathered = jax.tree.map(
        lambda a, kind: lax.all_gather(a.astype(kind), axis),
        shard,
        jax.tree.map(lambda a: jnp.bfloat16 if a.dtype == jnp.float32 else a.dtype, shard),
    )
    state = jax.tree.map(lambda a, e: jnp.zeros_like(a) + jnp.asarray(e, a.dtype), shard, neutral)

    def one(hop, state):
        return join(
            state,
            jax.tree.map(
                lambda a, own: lax.dynamic_index_in_dim(a, hop, 0, False).astype(own.dtype),
                gathered,
                shard,
            ),
        )

    return lax.fori_loop(0, place, one, state)


def from_behind(shard, axis, by):
    peers = lax.axis_size(axis)
    return lax.ppermute(shard, axis, [(i, (i + by) % peers) for i in range(peers)])


def rms(values, gain):
    return values * lax.rsqrt(jnp.mean(values * values, axis=-1, keepdims=True) + 1e-06) * gain


def unit_lower_solve(strict_part, rhs):
    ein = partial(jnp.einsum, precision=lax.Precision.HIGHEST)
    length = strict_part.shape[-1]
    raised = -strict_part
    running = jnp.eye(length, dtype=jnp.float32) + raised
    for _ in range((length - 1).bit_length() - 1):
        raised = ein("hij,hjk->hik", raised, raised)
        running = running + ein("hij,hjk->hik", running, raised)
    return ein("hij,hjk->hik", running, rhs)


def span_terms(lookup_vectors, values, beta, logd):
    ein = partial(jnp.einsum, precision=lax.Precision.HIGHEST)
    length = lookup_vectors.shape[1]
    dim_k = lookup_vectors.shape[2]
    cumul = jnp.cumsum(logd, axis=-1)
    posit = jnp.arange(length)
    strict = posit[:, None] > posit[None, :]
    differ = cumul[:, :, None] - cumul[:, None, :]
    ratio = jnp.where(strict, jnp.exp(jnp.where(strict, differ, 0.0)), 0.0)
    inner = ein("htd,hsd->hts", lookup_vectors, lookup_vectors)
    strict_part = beta[:, :, None] * ratio * inner
    growth = jnp.exp(cumul)
    rhs = jnp.concatenate(
        [(beta * growth)[:, :, None] * lookup_vectors, beta[:, :, None] * values], axis=-1
    )
    solved = unit_lower_solve(strict_part, rhs)
    w_part = solved[..., :dim_k]
    u_part = solved[..., dim_k:]
    tail = jnp.exp(cumul[:, -1:] - cumul)
    scaled = tail[:, :, None] * lookup_vectors
    trans_a = growth[:, -1][:, None, None] * jnp.eye(dim_k, dtype=jnp.float32) - ein(
        "hck,hcj->hkj", w_part, scaled
    )
    trans_b = ein("hcv,hck->hvk", u_part, scaled)
    return (cumul, w_part, u_part, trans_a, trans_b)


def span_output(queries, lookup_vectors, cumul, w_part, u_part, state):
    ein = partial(jnp.einsum, precision=lax.Precision.HIGHEST)
    length = lookup_vectors.shape[1]
    posit = jnp.arange(length)
    incl = posit[:, None] >= posit[None, :]
    differ = cumul[:, :, None] - cumul[:, None, :]
    ratio = jnp.where(incl, jnp.exp(jnp.where(incl, differ, 0.0)), 0.0)
    update = u_part - ein("hck,hvk->hcv", w_part, state)
    scores = ein("htd,hsd->hts", queries, lookup_vectors) * ratio
    return jnp.exp(cumul)[:, :, None] * ein("hck,hvk->hcv", queries, state) + ein(
        "hts,hsv->htv", scores, update
    )


def compose(earlier, later):
    ein = partial(jnp.einsum, precision=lax.Precision.HIGHEST)
    return (
        ein("hij,hjk->hik", earlier[0], later[0]),
        ein("hvk,hkj->hvj", earlier[1], later[0]) + later[1],
    )


def group_gather(piece, place):
    for bit in range(EXPERTS.bit_length() - 1):
        other = swapped(piece, "seq", bit)
        upper = place >> bit & 1
        piece = jnp.where(
            upper == 1,
            jnp.concatenate([other, piece], axis=0),
            jnp.concatenate([piece, other], axis=0),
        )
    return piece


def slice_gather(piece, place, low_bits, high_bits):
    for bit in range(high_bits):
        other = swapped(piece, "seq", low_bits + bit)
        upper = place >> low_bits + bit & 1
        piece = jnp.where(
            upper == 1,
            jnp.concatenate([other, piece], axis=0),
            jnp.concatenate([piece, other], axis=0),
        )
    return piece


def per_device(
    held,
    log_decay,
    route_ids,
    norm_gain,
    qkv_weight,
    beta_weight,
    out_gain,
    out_weight,
    ffn_gain,
    gate_weight,
    up_weight,
    down_weight,
):
    x_rows = held[0]
    steps_dev = x_rows.shape[0]
    width = x_rows.shape[1]
    heads = log_decay.shape[2]
    head_dim = width // heads
    xf = x_rows.astype(jnp.float32)
    xn = rms(xf, norm_gain[0]).astype(jnp.bfloat16)
    qkv = (
        jnp.dot(xn, qkv_weight[0], preferred_element_type=jnp.float32)
        .astype(jnp.bfloat16)
        .astype(jnp.float32)
    )
    queries = qkv[:, :width].reshape(steps_dev, heads, head_dim)
    lookup_vectors = qkv[:, width : 2 * width].reshape(steps_dev, heads, head_dim)
    values = qkv[:, 2 * width :].reshape(steps_dev, heads, head_dim)
    queries = queries * lax.rsqrt(jnp.sum(queries * queries, axis=-1, keepdims=True) + 1e-06)
    lookup_vectors = lookup_vectors * lax.rsqrt(
        jnp.sum(lookup_vectors * lookup_vectors, axis=-1, keepdims=True) + 1e-06
    )
    beta = jax.nn.sigmoid(jnp.dot(xn, beta_weight[0], preferred_element_type=jnp.float32))
    spans = steps_dev // BLOCK

    def arrange(arr):
        return arr.reshape(spans, BLOCK, heads, head_dim).transpose(0, 2, 1, 3)

    q_c = arrange(queries)
    k_c = arrange(lookup_vectors)
    v_c = arrange(values)
    b_c = beta.reshape(spans, BLOCK, heads).transpose(0, 2, 1)
    l_c = log_decay[0].reshape(spans, BLOCK, heads).transpose(0, 2, 1)
    terms = span_terms(k_c[0], v_c[0], b_c[0], l_c[0])
    total_pair = (terms[3], terms[4])
    identity = (
        jnp.broadcast_to(jnp.eye(head_dim, dtype=jnp.float32), (heads, head_dim, head_dim)),
        jnp.zeros((heads, head_dim, head_dim), jnp.float32),
    )
    prefix = carried_in(total_pair, "seq", compose, identity)
    state = prefix[1]
    cumul, w_part, u_part, trans_a, trans_b = terms
    results = [span_output(q_c[0], k_c[0], cumul, w_part, u_part, state)]
    mixed = jnp.stack(results, axis=0).transpose(0, 2, 1, 3).reshape(steps_dev, heads, head_dim)
    normed = rms(mixed, out_gain[0]).astype(jnp.bfloat16).reshape(steps_dev, width)
    hidden = (xf + jnp.dot(normed, out_weight[0], preferred_element_type=jnp.float32)).astype(
        jnp.bfloat16
    )
    hn = rms(hidden.astype(jnp.float32), ffn_gain[0]).astype(jnp.bfloat16)
    place = lax.axis_index("seq")
    low_bits = EXPERTS.bit_length() - 1
    high_bits = lax.axis_size("seq").bit_length() - 1 - low_bits
    own_kind = place % EXPERTS
    group = place // EXPERTS
    blocks_dev = steps_dev // BLOCK
    group_size = EXPERTS * blocks_dev
    capacity = 2 * blocks_dev
    kinds = route_ids[0, :, 0]
    group_kinds = lax.dynamic_slice_in_dim(kinds, group * group_size, group_size)
    index_g = jnp.arange(group_size)
    same = group_kinds[:, None] == group_kinds[None, :]
    before = index_g[None, :] < index_g[:, None]
    rank_all = jnp.sum((same & before).astype(jnp.int32), axis=1)
    slot_ids = jnp.arange(capacity)
    select = ((group_kinds[None, :] == own_kind) & (rank_all[None, :] == slot_ids[:, None])).astype(
        jnp.bfloat16
    )
    grouped = group_gather(hn.reshape(blocks_dev, BLOCK, width), place)
    picked = jnp.einsum("cb,brd->crd", select, grouped, preferred_element_type=jnp.float32).astype(
        jnp.bfloat16
    )
    spread = slice_gather(picked, place, low_bits, high_bits)
    rows = spread.reshape(-1, width)
    gate = jnp.dot(rows, gate_weight[0, 0], preferred_element_type=jnp.float32)
    up_val = jnp.dot(rows, up_weight[0, 0], preferred_element_type=jnp.float32)
    act = (jax.nn.silu(gate) * up_val).astype(jnp.bfloat16)
    partial_sum = jnp.dot(act, down_weight[0, 0], preferred_element_type=jnp.float32)
    buffer = partial_sum.reshape(-1, capacity * BLOCK, width)
    for bit in reversed(range(high_bits)):
        half = buffer.shape[0] // 2
        lower_half = buffer[:half]
        upper_half = buffer[half:]
        upper = group >> bit & 1
        keep = jnp.where(upper == 1, upper_half, lower_half)
        send = jnp.where(upper == 1, lower_half, upper_half)
        buffer = keep + swapped(send.astype(jnp.bfloat16), "seq", low_bits + bit).astype(send.dtype)
    finished = buffer[0].astype(jnp.bfloat16).reshape(capacity, BLOCK, width)
    returned = group_gather(finished, place)
    mine = own_kind * blocks_dev + jnp.arange(blocks_dev)
    target = jnp.take(group_kinds, mine) * capacity + jnp.take(rank_all, mine)
    choose = (jnp.arange(EXPERTS * capacity)[None, :] == target[:, None]).astype(jnp.bfloat16)
    ffn = (
        jnp.einsum("ib,brd->ird", choose, returned, preferred_element_type=jnp.float32)
        .astype(jnp.bfloat16)
        .reshape(steps_dev, width)
    )
    result = (hidden.astype(jnp.float32) + ffn.astype(jnp.float32)).astype(jnp.bfloat16)
    moved = from_behind(result, "segment", 1)
    return moved[None]


def solution(mesh):
    placed = (
        P("segment", "seq", None),
        P("segment", "seq", None),
        P("segment", None, None),
        P("segment", None),
        P("segment", None, None),
        P("segment", None, None),
        P("segment", None),
        P("segment", None, None),
        P("segment", None),
        P("segment", "seq", None, None),
        P("segment", "seq", None, None),
        P("segment", "seq", None, None),
    )
    return jax.shard_map(
        per_device, mesh=mesh, in_specs=placed, out_specs=P("segment", "seq", None), check_vma=False
    )
```

profile of v0, /device:TPU:96, one launch (start us, length us, event | category | flops | bytes accessed | tf_op | source)
XLA Modules:
  0.0 847.4 jit_solution(4011545663990171834)
XLA Ops:
  10.4 4.0 fusion.11
  39.7 91.9 %all-gather.5.cloned.1.call-done = bf16[512,128,128]{2,1,0:T(8,128)(2,1)} async-done(((bf16[8,128,128]{2,1,0:T(8,128)(2,1)}), bf16[512,128,128]{2,1,0:T(8,128)(2,1)}) %all-gather.5.cloned.1.call-update) | async-done | bytes 16777232 | tf_op jit(solution)/shard_map/all_gather | solution.py:25
  131.7 99.0 %all-gather.7.cloned.1.call-done = bf16[512,128,128]{2,1,0:T(8,128)(2,1)} async-done(((bf16[8,128,128]{2,1,0:T(8,128)(2,1)}), bf16[512,128,128]{2,1,0:T(8,128)(2,1)}) %all-gather.7.cloned.1.call-update) | async-done | bytes 16777232 | tf_op jit(solution)/shard_map/all_gather | solution.py:25
  230.7 15.8 %while.14 = (s32[]{:T(128)}, f32[8,128,128]{1,2,0:T(8,128)S(1)}, s32[]{:T(128)}, bf16[64,8,128,128]{3,2,1,0:T(8,128)(2,1)}, bf16[64,8,128,128]{3,2,1,0:T(8,128)(2,1)}, /*index=5*/s32[]{:T(128)}, s32[]{:T(128)}, s32[]{:T(128)}) while((s32[]{:T(128)}, f32[8,128,128]{1,2,0:T(8,128)S(1)}, s32[]{:T(128)}, bf16[64,8,128,128]{3,2,1,0:T(8,128)(2,1)}, ...), condition=%wide.region_5.6_spmd, body=%wide.region_4.5_spmd.sunk | while | flops 201588736 | bytes 3670151 | solution.py:41
  258.0 14.2 %collective-permute-done.1 = bf16[2,128,1024]{2,1,0:T(8,128)(2,1)S(1)} collective-permute-done((bf16[2,128,1024]{2,1,0:T(8,128)(2,1)S(1)}, bf16[2,128,1024]{2,1,0:T(8,128)(2,1)S(1)}, u32[]{:S(2)}, u32[]{:S(2)}) %collective-permute-start.1) | collective-permute-done | bytes 524320 | tf_op jit(solution)/shard_map/ppermute | solution.py:19
  273.3 47.4 %collective-permute-done.2 = bf16[4,128,1024]{2,1,0:T(8,128)(2,1)} collective-permute-done((bf16[4,128,1024]{2,1,0:T(8,128)(2,1)S(1)}, bf16[4,128,1024]{2,1,0:T(8,128)(2,1)}, u32[]{:S(2)}, u32[]{:S(2)}) %collective-permute-start.2) | collective-permute-done | bytes 1048608 | tf_op jit(solution)/shard_map/ppermute | solution.py:19
  324.7 22.9 %collective-permute-start.3 = (bf16[2,128,1024]{2,0,1:T(2,128)(2,1)S(1)}, bf16[2,128,1024]{2,0,1:T(2,128)(2,1)S(1)}, u32[]{:S(2)}, u32[]{:S(2)}) collective-permute-start(bf16[2,128,1024]{2,0,1:T(2,128)(2,1)S(1)} %fusion.19), channel_id=1, source_target_pairs={{0,8},{8,0},{1,9},{9,1},{2,10},{10,2},{3,11},{11,3},{4,12},{12,4},... | collective-permute-start | bytes 1572872 | tf_op jit(solution)/shard_map/ppermute | solution.py:19
  347.6 23.5 %collective-permute-done.3 = bf16[2,128,1024]{2,0,1:T(2,128)(2,1)S(1)} collective-permute-done((bf16[2,128,1024]{2,0,1:T(2,128)(2,1)S(1)}, bf16[2,128,1024]{2,0,1:T(2,128)(2,1)S(1)}, u32[]{:S(2)}, u32[]{:S(2)}) %collective-permute-start.3) | collective-permute-done | bytes 524320 | tf_op jit(solution)/shard_map/ppermute | solution.py:19
  373.0 42.5 %collective-permute-start.4 = (bf16[4,128,1024]{2,0,1:T(4,128)(2,1)S(1)}, bf16[4,128,1024]{2,0,1:T(4,128)(2,1)}, u32[]{:S(2)}, u32[]{:S(2)}) collective-permute-start(bf16[4,128,1024]{2,0,1:T(4,128)(2,1)S(1)} %maximum_select_fusion.6), channel_id=1, source_target_pairs={{0,16},{16,0},{1,17},{17,1},{2,18},{18,2},{3,19},{19,3},{4,20},{20... | collective-permute-start | bytes 3145736 | tf_op jit(solution)/shard_map/ppermute | solution.py:19
  415.5 22.8 %collective-permute-done.4 = bf16[4,128,1024]{2,0,1:T(4,128)(2,1)} collective-permute-done((bf16[4,128,1024]{2,0,1:T(4,128)(2,1)S(1)}, bf16[4,128,1024]{2,0,1:T(4,128)(2,1)}, u32[]{:S(2)}, u32[]{:S(2)}) %collective-permute-start.4) | collective-permute-done | bytes 1048608 | tf_op jit(solution)/shard_map/ppermute | solution.py:19
  438.3 4.3 maximum_select_fusion.3
  442.6 87.0 %collective-permute-start.5 = (bf16[8,128,1024]{2,0,1:T(8,128)(2,1)S(1)}, bf16[8,128,1024]{2,0,1:T(8,128)(2,1)}, u32[]{:S(2)}, u32[]{:S(2)}) collective-permute-start(bf16[8,128,1024]{2,0,1:T(8,128)(2,1)S(1)} %maximum_select_fusion.3), channel_id=1, source_target_pairs={{0,32},{32,0},{1,33},{33,1},{2,34},{34,2},{3,35},{35,3},{4,36},{36... | collective-permute-start | bytes 6291464 | tf_op jit(solution)/shard_map/ppermute | solution.py:19
  529.6 44.7 %collective-permute-done.5 = bf16[8,128,1024]{2,0,1:T(8,128)(2,1)} collective-permute-done((bf16[8,128,1024]{2,0,1:T(8,128)(2,1)S(1)}, bf16[8,128,1024]{2,0,1:T(8,128)(2,1)}, u32[]{:S(2)}, u32[]{:S(2)}) %collective-permute-start.5) | collective-permute-done | bytes 2097184 | tf_op jit(solution)/shard_map/ppermute | solution.py:19
  574.3 4.5 maximum_select_fusion
  583.1 4.4 fusion.45
  587.5 12.0 %fusion.18 = f32[2048,1024]{1,0:T(8,128)} fusion(f32[2048,512]{1,0:T(8,128)} %fusion.45, bf16[2048,1024]{1,0:T(8,128)(2,1)} %bitcast.190, bf16[1,1,512,1024]{3,2,1,0:T(8,128)(2,1)S(1)} %copy-done.14, bf16[1,1,1024,512]{3,2,1,0:T(8,128)(2,1)} %param.24), kind=kOutput, calls=%fused_computation.27 | convolution fusion | flops 4301258752 | bytes 18874368 | tf_op jit(solution)/shard_map/dot_general | solution.py:224
  599.5 5.2 select_convert_fusion
  608.1 4.4 slice_select_fusion
  612.5 39.8 %collective-permute-done.6 = bf16[4,256,1024]{2,1,0:T(8,128)(2,1)S(1)} collective-permute-done((bf16[4,256,1024]{2,1,0:T(8,128)(2,1)}, bf16[4,256,1024]{2,1,0:T(8,128)(2,1)S(1)}, u32[]{:S(2)}, u32[]{:S(2)}) %collective-permute-start.6) | collective-permute-done | bytes 2097184 | tf_op jit(solution)/shard_map/ppermute | solution.py:19
  656.2 22.0 %collective-permute-done.7 = bf16[2,256,1024]{2,1,0:T(8,128)(2,1)} collective-permute-done((bf16[2,256,1024]{2,1,0:T(8,128)(2,1)S(1)}, bf16[2,256,1024]{2,1,0:T(8,128)(2,1)}, u32[]{:S(2)}, u32[]{:S(2)}) %collective-permute-start.7) | collective-permute-done | bytes 1048608 | tf_op jit(solution)/shard_map/ppermute | solution.py:19
  683.0 19.6 %collective-permute-done.8 = bf16[1,256,1024]{2,1,0:T(8,128)(2,1)S(1)} collective-permute-done((bf16[1,256,1024]{2,1,0:T(8,128)(2,1)S(1)}, bf16[1,256,1024]{2,1,0:T(8,128)(2,1)S(1)}, u32[]{:S(2)}, u32[]{:S(2)}) %collective-permute-start.8) | collective-permute-done | bytes 524320 | tf_op jit(solution)/shard_map/ppermute | solution.py:19
  705.2 25.2 %collective-permute-done.10 = bf16[4,128,1024]{2,1,0:T(8,128)(2,1)S(1)} collective-permute-done((bf16[4,128,1024]{2,1,0:T(8,128)(2,1)S(1)}, bf16[4,128,1024]{2,1,0:T(8,128)(2,1)S(1)}, u32[]{:S(2)}, u32[]{:S(2)}) %collective-permute-start.10) | collective-permute-done | bytes 1048608 | tf_op jit(solution)/shard_map/ppermute | solution.py:19
  733.3 90.2 %collective-permute-done.11 = bf16[8,128,1024]{2,1,0:T(8,128)(2,1)} collective-permute-done((bf16[8,128,1024]{2,1,0:T(8,128)(2,1)S(1)}, bf16[8,128,1024]{2,1,0:T(8,128)(2,1)}, u32[]{:S(2)}, u32[]{:S(2)}) %collective-permute-start.11) | collective-permute-done | bytes 2097184 | tf_op jit(solution)/shard_map/ppermute | solution.py:19
  831.7 7.9 collective-permute-done.12
  (139 shorter events, 92.3 us)
Async XLA Ops:
  6.5 246.4 %copy-start = (bf16[1,1024,1024]{2,1,0:T(8,128)(2,1)S(1)}, bf16[1,1024,1024]{2,1,0:T(8,128)(2,1)}, u32[]{:S(2)}) copy-start(bf16[1,1024,1024]{2,1,0:T(8,128)(2,1)} %param.21) | copy-start | bytes 6291460
  6.5 125.1 %all-gather.5.cloned.1.call-start = ((), (), s32[]{:S(2)}) async-start(), calls=%async_computation | async-start | bytes 17039360 | tf_op jit(solution)/shard_map/all_gather | solution.py:25
  31.1 199.6 %all-gather.7.cloned.1.call-start = ((), (), s32[]{:S(2)}) async-start(), calls=%async_computation.1 | async-start | bytes 17039360 | tf_op jit(solution)/shard_map/all_gather | solution.py:25
  246.6 6.3 copy-start.12
  246.6 6.4 copy-start.9
  248.5 5.1 copy-start.10
  252.8 19.9 %copy-start.11 = (s32[1,64,1]{1,2,0:T(1,128)S(1)}, s32[1,64,1]{1,2,0:T(1,128)}, u32[]{:S(2)}) copy-start(s32[1,64,1]{1,2,0:T(1,128)} %param.16) | copy-start | bytes 772
  253.7 4.1 collective-permute-start
  257.9 14.3 %collective-permute-start.1 = (bf16[2,128,1024]{2,1,0:T(8,128)(2,1)S(1)}, bf16[2,128,1024]{2,1,0:T(8,128)(2,1)S(1)}, u32[]{:S(2)}, u32[]{:S(2)}) collective-permute-start(bf16[2,128,1024]{2,1,0:T(8,128)(2,1)S(1)} %maximum_select_fusion.8), channel_id=1, source_target_pairs={{0,2},{2,0},{1,3},{3,1},{4,6},{6,4},{5,7},{7,5},{8,10},{10,8},{9,1... | collective-permute-start | bytes 1572872 | tf_op jit(solution)/shard_map/ppermute | solution.py:19
  272.4 48.4 %collective-permute-start.2 = (bf16[4,128,1024]{2,1,0:T(8,128)(2,1)S(1)}, bf16[4,128,1024]{2,1,0:T(8,128)(2,1)}, u32[]{:S(2)}, u32[]{:S(2)}) collective-permute-start(bf16[4,128,1024]{2,1,0:T(8,128)(2,1)S(1)} %maximum_select_fusion.5), channel_id=1, source_target_pairs={{0,4},{4,0},{1,5},{5,1},{2,6},{6,2},{3,7},{7,3},{8,12},{12,8},{9,1... | collective-permute-start | bytes 3145736 | tf_op jit(solution)/shard_map/ppermute | solution.py:19
  324.7 46.4 %collective-permute-start.3 = (bf16[2,128,1024]{2,0,1:T(2,128)(2,1)S(1)}, bf16[2,128,1024]{2,0,1:T(2,128)(2,1)S(1)}, u32[]{:S(2)}, u32[]{:S(2)}) collective-permute-start(bf16[2,128,1024]{2,0,1:T(2,128)(2,1)S(1)} %fusion.19), channel_id=1, source_target_pairs={{0,8},{8,0},{1,9},{9,1},{2,10},{10,2},{3,11},{11,3},{4,12},{12,4},... | collective-permute-start | bytes 1572872 | tf_op jit(solution)/shard_map/ppermute | solution.py:19
  373.0 42.5 %copy-start.7 = (bf16[4,128,1024]{2,0,1:T(4,128)(2,1)}, bf16[4,128,1024]{2,0,1:T(4,128)(2,1)S(1)}, u32[]{:S(2)}) copy-start(bf16[4,128,1024]{2,0,1:T(4,128)(2,1)S(1)} %maximum_select_fusion.6) | copy-start | bytes 3145732
  373.0 65.3 %collective-permute-start.4 = (bf16[4,128,1024]{2,0,1:T(4,128)(2,1)S(1)}, bf16[4,128,1024]{2,0,1:T(4,128)(2,1)}, u32[]{:S(2)}, u32[]{:S(2)}) collective-permute-start(bf16[4,128,1024]{2,0,1:T(4,128)(2,1)S(1)} %maximum_select_fusion.6), channel_id=1, source_target_pairs={{0,16},{16,0},{1,17},{17,1},{2,18},{18,2},{3,19},{19,3},{4,20},{20... | collective-permute-start | bytes 3145736 | tf_op jit(solution)/shard_map/ppermute | solution.py:19
  442.6 131.7 %collective-permute-start.5 = (bf16[8,128,1024]{2,0,1:T(8,128)(2,1)S(1)}, bf16[8,128,1024]{2,0,1:T(8,128)(2,1)}, u32[]{:S(2)}, u32[]{:S(2)}) collective-permute-start(bf16[8,128,1024]{2,0,1:T(8,128)(2,1)S(1)} %maximum_select_fusion.3), channel_id=1, source_target_pairs={{0,32},{32,0},{1,33},{33,1},{2,34},{34,2},{3,35},{35,3},{4,36},{36... | collective-permute-start | bytes 6291464 | tf_op jit(solution)/shard_map/ppermute | solution.py:19
  578.8 4.3 copy-start.13
  583.1 4.4 copy-start.14
  604.7 47.6 %collective-permute-start.6 = (bf16[4,256,1024]{2,1,0:T(8,128)(2,1)}, bf16[4,256,1024]{2,1,0:T(8,128)(2,1)S(1)}, u32[]{:S(2)}, u32[]{:S(2)}) collective-permute-start(bf16[4,256,1024]{2,1,0:T(8,128)(2,1)} %bitcast.45), channel_id=1, source_target_pairs={{0,32},{32,0},{1,33},{33,1},{2,34},{34,2},{3,35},{35,3},{4,36},{36... | collective-permute-start | bytes 6291464 | tf_op jit(solution)/shard_map/ppermute | solution.py:19
  655.5 22.6 %collective-permute-start.7 = (bf16[2,256,1024]{2,1,0:T(8,128)(2,1)S(1)}, bf16[2,256,1024]{2,1,0:T(8,128)(2,1)}, u32[]{:S(2)}, u32[]{:S(2)}) collective-permute-start(bf16[2,256,1024]{2,1,0:T(8,128)(2,1)S(1)} %select_convert_fusion.1), channel_id=1, source_target_pairs={{0,16},{16,0},{1,17},{17,1},{2,18},{18,2},{3,19},{19,3},{4,20},{20... | collective-permute-start | bytes 3145736 | tf_op jit(solution)/shard_map/ppermute | solution.py:19
  681.5 21.1 %collective-permute-start.8 = (bf16[1,256,1024]{2,1,0:T(8,128)(2,1)S(1)}, bf16[1,256,1024]{2,1,0:T(8,128)(2,1)S(1)}, u32[]{:S(2)}, u32[]{:S(2)}) collective-permute-start(bf16[1,256,1024]{2,1,0:T(8,128)(2,1)S(1)} %select_convert_fusion.2), channel_id=1, source_target_pairs={{0,8},{8,0},{1,9},{9,1},{2,10},{10,2},{3,11},{11,3},{4,12},{12,4},... | collective-permute-start | bytes 1572872 | tf_op jit(solution)/shard_map/ppermute | solution.py:19
  702.9 2.0 collective-permute-start.9
  705.1 25.3 %collective-permute-start.10 = (bf16[4,128,1024]{2,1,0:T(8,128)(2,1)S(1)}, bf16[4,128,1024]{2,1,0:T(8,128)(2,1)S(1)}, u32[]{:S(2)}, u32[]{:S(2)}) collective-permute-start(bf16[4,128,1024]{2,1,0:T(8,128)(2,1)S(1)} %maximum_select_fusion.7), channel_id=1, source_target_pairs={{0,2},{2,0},{1,3},{3,1},{4,6},{6,4},{5,7},{7,5},{8,10},{10,8},{9,1... | collective-permute-start | bytes 3145736 | tf_op jit(solution)/shard_map/ppermute | solution.py:19
  730.7 92.8 %collective-permute-start.11 = (bf16[8,128,1024]{2,1,0:T(8,128)(2,1)S(1)}, bf16[8,128,1024]{2,1,0:T(8,128)(2,1)}, u32[]{:S(2)}, u32[]{:S(2)}) collective-permute-start(bf16[8,128,1024]{2,1,0:T(8,128)(2,1)S(1)} %maximum_select_fusion.4), channel_id=1, source_target_pairs={{0,4},{4,0},{1,5},{5,1},{2,6},{6,2},{3,7},{7,3},{8,12},{12,8},{9,1... | collective-permute-start | bytes 6291464 | tf_op jit(solution)/shard_map/ppermute | solution.py:19
  823.6 16.8 %copy-start.1 = (bf16[1,1024,1024]{2,1,0:T(8,128)(2,1)S(1)}, bf16[1,1024,1024]{2,1,0:T(8,128)(2,1)}, u32[]{:S(2)}) copy-start(bf16[1,1024,1024]{2,1,0:T(8,128)(2,1)} %param.21) | copy-start | bytes 6291460
  830.1 9.5 %collective-permute-start.12 = (bf16[128,1024]{1,0:T(8,128)(2,1)S(1)}, bf16[128,1024]{1,0:T(8,128)(2,1)S(1)}, u32[]{:S(2)}, u32[]{:S(2)}) collective-permute-start(bf16[128,1024]{1,0:T(8,128)(2,1)S(1)} %add_convert_fusion.1), channel_id=1, source_target_pairs={{0,64},{64,128},{128,192},{192,0},{1,65},{65,129},{129,193},{193,1... | collective-permute-start | bytes 786440 | tf_op jit(solution)/shard_map/ppermute | solution.py:46
  (6 other events, 9.3 us)
Sparse Core Ops, SparseCore 0:
  31.2 100.4 all-gather.4
  134.5 96.1 all-gather.6
where the time goes:
time: 860 us; the launch traced here: 847 us
  waiting for transfers between devices  551 us (64%)
  starting transfers between devices  163 us (19%)
  matrix products  58.1 us (7%)
  other arithmetic  37.3 us (4%)
  local copies, waits for them, and re-layouts  21.7 us (3%)
  between operations  15.4 us (2%)
    ppermute x12, waiting for transfers between devices, swapped(): return lax.ppermute(block, axis, route)  352 us
    all_gather x2, waiting for transfers between devices, carried_in(): lax.all_gather(a.astype(kind), axis)  191 us
    ppermute x12, starting transfers between devices, swapped(): return lax.ppermute(block, axis, route)  162 us
  transfers between devices with their start and end apart: 15, of which 15 were waited for; matrix products, arithmetic and copies ran while one was open for 2% of the time, Pallas kernels for 0%

commit v1 on v0

v1 whole, which is shorter than its diff:
```python
from functools import partial

import jax
import jax.numpy as jnp
from jax import lax
from jax.experimental import pallas as pl
from jax.experimental.pallas import tpu as pltpu
from jax.sharding import PartitionSpec as P

EXPERTS = 8


def rms(values, gain):
    return values * lax.rsqrt(jnp.mean(values * values, axis=-1, keepdims=True) + 1e-06) * gain


def unit_lower_solve(strict_part, rhs):
    ein = partial(jnp.einsum, precision=lax.Precision.HIGHEST)
    length = strict_part.shape[-1]
    raised = -strict_part
    running = jnp.eye(length, dtype=jnp.float32) + raised
    for _ in range((length - 1).bit_length() - 1):
        raised = ein("hij,hjk->hik", raised, raised)
        running = running + ein("hij,hjk->hik", running, raised)
    return ein("hij,hjk->hik", running, rhs)


def span_terms(lookup_vectors, values, beta, logd):
    ein = partial(jnp.einsum, precision=lax.Precision.HIGHEST)
    length = lookup_vectors.shape[1]
    dim_k = lookup_vectors.shape[2]
    cumul = jnp.cumsum(logd, axis=-1)
    posit = jnp.arange(length)
    strict = posit[:, None] > posit[None, :]
    differ = cumul[:, :, None] - cumul[:, None, :]
    ratio = jnp.where(strict, jnp.exp(jnp.where(strict, differ, 0.0)), 0.0)
    inner = ein("htd,hsd->hts", lookup_vectors, lookup_vectors)
    strict_part = beta[:, :, None] * ratio * inner
    growth = jnp.exp(cumul)
    rhs = jnp.concatenate(
        [(beta * growth)[:, :, None] * lookup_vectors, beta[:, :, None] * values], axis=-1
    )
    solved = unit_lower_solve(strict_part, rhs)
    w_part = solved[..., :dim_k]
    u_part = solved[..., dim_k:]
    tail = jnp.exp(cumul[:, -1:] - cumul)
    scaled = tail[:, :, None] * lookup_vectors
    trans_a = growth[:, -1][:, None, None] * jnp.eye(dim_k, dtype=jnp.float32) - ein(
        "hck,hcj->hkj", w_part, scaled
    )
    trans_b = ein("hcv,hck->hvk", u_part, scaled)
    return (cumul, w_part, u_part, trans_a, trans_b)


LEG = ("segment", "seq")
MESH = pl.DeviceIdType.MESH
NCH = 4
CW = 256
F32 = jnp.float32
BF16 = jnp.bfloat16


def hdot(a, b):
    return jnp.dot(a, b, precision=lax.Precision.HIGHEST, preferred_element_type=F32)


def tick_kernel(
    sel_ref, tgt_ref, ab_ref, qp_ref, o0_ref, x_ref, og_ref, wo_ref, fg_ref,
    gate_hbm, up_hbm, down_hbm,
    out_ref,
    ab_in, tp, tot_out, tot_in, s_out, s_in, on, hid, gath, xs, wg, wu, wd, act, part,
    pout, pin, sr, sl, rr, rl, yout, entering,
    lsem, a2a_s, a2a_r, tot_s, tot_r, st_s, st_r, w_s, w_r, ag_s, ag_r, pf_s, pf_r,
    px_s, px_r, rr_s, rr_r, rl_s, rl_r, y_s, y_r,
):
    seg = lax.axis_index("segment")
    me = lax.axis_index("seq")
    col = me // 16
    z = lax.rem(me // 2, 8)
    core = lax.rem(me, 2)
    grp = me // 8
    i = lax.rem(me, 8)

    def at(xx, zz, cc):
        return (seg, (xx * 8 + zz) * 2 + cc)

    def remote(src, dst, ssem, rsem, dev):
        return pltpu.make_async_remote_copy(
            src_ref=src, dst_ref=dst, send_sem=ssem, recv_sem=rsem,
            device_id=dev, device_id_type=MESH,
        )

    right = at(col, lax.rem(z + 1, 8), core)
    left = at(col, lax.rem(z + 7, 8), core)
    mate = at(col, z, 1 - core)
    xr = at(lax.rem(col + 1, 4), z, core)
    xl = at(lax.rem(col + 3, 4), z, core)
    yn = (lax.rem(seg + 1, 4), me)
    yp = (lax.rem(seg + 3, 4), me)

    barrier = pltpu.get_barrier_semaphore()
    for k in range(1, 8):
        pl.semaphore_signal(barrier, inc=1, device_id=(seg, grp * 8 + lax.rem(i + k, 8)), device_id_type=MESH)
        pl.semaphore_signal(barrier, inc=1, device_id=(seg, lax.rem(grp + k, 8) * 8 + i), device_id_type=MESH)
    for d in (right, left, yn, yp):
        pl.semaphore_signal(barrier, inc=1, device_id=d, device_id_type=MESH)
    pl.semaphore_wait(barrier, 18)

    def a2a_copy(h):
        return remote(ab_ref.at[h], ab_in.at[i], a2a_s.at[h], a2a_r.at[i], (seg, grp * 8 + h))

    def a2a_from(j):
        return remote(ab_ref.at[j], ab_in.at[j], a2a_s.at[j], a2a_r.at[j], (seg, grp * 8 + j))

    @pl.loop(1, 8)
    def _(k):
        a2a_copy(lax.rem(i + k, 8)).start()

    xleft, xright = lax.rem(col + 3, 4), lax.rem(col + 1, 4)
    hbms = (gate_hbm, up_hbm, down_hbm)
    bufs = (wg, wu, wd)

    def piece(buf, k):
        rows = 512 if k // 2 < 2 else 256
        return buf.at[pl.ds((k % 2) * rows, rows)]

    def w_own(k, way):
        a = k // 2
        return remote(
            piece(hbms[a], k), piece(bufs[a].at[col], k), w_s.at[way, k], w_r.at[way, k],
            xr if way == 0 else xl,
        )

    relay_of = ((0, 1, 4), (2, 3, 5))

    def w_relay(r, way):
        k = relay_of[way][r]
        a = k // 2
        origin = xleft if way == 0 else xright
        return remote(
            piece(bufs[a].at[origin], k), piece(bufs[a].at[origin], k),
            w_s.at[way, 6 + r], w_r.at[way, 6 + r], xr if way == 0 else xl,
        )

    def w_got(k, way):
        w_own(k, way).wait_recv()

    w_own(0, 0).start()
    w_own(0, 1).start()
    locals_ = [pltpu.make_async_copy(hbms[a], bufs[a].at[col], lsem.at[a]) for a in range(3)]
    for c in locals_:
        c.start()

    ab_in[i] = ab_ref[i]

    @pl.when(i != 0)
    def _():
        a2a_from(0).wait_recv()

    rows = lax.broadcasted_iota(jnp.int32, (256, 128), 0)
    cols = lax.broadcasted_iota(jnp.int32, (256, 128), 1)
    tp[0] = jnp.where(rows == cols, 1.0, 0.0).astype(F32)
    tp[1] = ab_in[0].astype(F32)

    @pl.loop(1, 8)
    def _(j):
        @pl.when(i != j)
        def _():
            a2a_from(j).wait_recv()

        low = ab_in[j].astype(F32)
        tp[j + 1] = hdot(tp[j], low[:128]) + jnp.where(rows >= 128, low, 0.0)

    tot_out[...] = tp[8].astype(BF16)

    def tot_copy(g):
        return remote(tot_out, tot_in.at[grp], tot_s.at[g], tot_r.at[grp], (seg, g * 8 + i))

    def tot_from(g):
        return remote(tot_out, tot_in.at[g], tot_s.at[g], tot_r.at[g], (seg, g * 8 + i))

    @pl.loop(grp + 1, 8)
    def _(g):
        tot_copy(g).start()

    entering[...] = jnp.zeros((128, 128), F32)

    @pl.loop(0, grp)
    def _(g):
        tot_from(g).wait_recv()
        pair = tot_in[g].astype(F32)
        entering[...] = hdot(entering[...], pair[:128]) + pair[128:]

    def st_copy(j):
        return remote(s_out.at[j], s_in.at[i], st_s.at[j], st_r.at[i], (seg, grp * 8 + j))

    def st_from(j):
        return remote(s_out.at[j], s_in.at[j], st_s.at[j], st_r.at[j], (seg, grp * 8 + j))

    @pl.loop(0, 8)
    def _(j):
        pre = tp[j]
        entered = (hdot(entering[...], pre[:128]) + pre[128:]).astype(BF16)
        s_out[j] = entered

        @pl.when(j == i)
        def _():
            s_in[j] = entered

        @pl.when(j != i)
        def _():
            st_copy(j).start()

    for k in range(1, 6):
        w_own(k, 0).start()
        w_own(k, 1).start()
    w_got(0, 0)
    w_relay(0, 0).start()
    w_got(0, 1)

    @pl.loop(0, 8)
    def _(h):
        @pl.when(h != i)
        def _():
            st_from(h).wait_recv()

        o = o0_ref[h] + lax.dot_general(
            qp_ref[h], s_in[h].astype(F32), (((1,), (1,)), ((), ())),
            precision=lax.Precision.HIGHEST, preferred_element_type=F32,
        )
        o = o * lax.rsqrt(jnp.mean(o * o, axis=-1, keepdims=True) + 1e-06) * og_ref[...]
        on[:, pl.ds(pl.multiple_of(h * 128, 128), 128)] = o.astype(BF16)

    hidden = (
        x_ref[...].astype(F32) + jnp.dot(on[...], wo_ref[...], preferred_element_type=F32)
    ).astype(BF16)
    hid[...] = hidden
    hf = hidden.astype(F32)
    hf = hf * lax.rsqrt(jnp.mean(hf * hf, axis=-1, keepdims=True) + 1e-06) * fg_ref[...]
    gath[me - col * 16] = hf.astype(BF16)

    def half(zz, hv):
        return gath.at[lax.rem(zz, 8) * 2 + core, pl.ds(hv * 64, 64)]

    def ag_send(s, hv, way):
        ref = half(z + 8 - s if way == 0 else z + s, hv)
        k = s * 2 + hv
        return remote(ref, ref, ag_s.at[way, k], ag_r.at[way, k], right if way == 0 else left)

    def ag_recv(s, hv, way):
        ref = half(z + 7 - s if way == 0 else z + 1 + s, hv)
        k = s * 2 + hv
        return remote(ref, ref, ag_s.at[way, k], ag_r.at[way, k], right if way == 0 else left)

    def mate_send(dz, hv):
        ref = half(z + dz, hv)
        k = dz * 2 + hv
        return remote(ref, ref, pf_s.at[k], pf_r.at[k], mate)

    def mate_recv(dz, hv):
        ref = gath.at[lax.rem(z + dz, 8) * 2 + 1 - core, pl.ds(hv * 64, 64)]
        k = dz * 2 + hv
        return remote(ref, ref, pf_s.at[k], pf_r.at[k], mate)

    for hv in range(2):
        for way in range(2):
            ag_send(0, hv, way).start()
    for hv in range(2):
        mate_send(0, hv).start()
    for s in range(1, 4):
        for hv in range(2):
            for way in range(2):
                ag_recv(s - 1, hv, way).wait_recv()
                if s < 3 or hv == way:
                    ag_send(s, hv, way).start()
                mate_send(8 - s if way == 0 else s, hv).start()
    w_got(1, 0)
    w_relay(1, 0).start()
    w_got(1, 1)
    w_got(2, 1)
    w_relay(0, 1).start()
    ag_recv(3, 0, 0).wait_recv()
    mate_send(4, 0).start()
    ag_recv(3, 1, 1).wait_recv()
    mate_send(4, 1).start()
    for dz in range(8):
        for hv in range(2):
            mate_recv(dz, hv).wait_recv()

    for k in range(4):
        xs[pl.ds(k * 128, 128)] = gath[sel_ref[k]]

    def hidden_units(src):
        @pl.loop(0, 2)
        def _(n):
            cut = pl.ds(pl.multiple_of(n * 256, 256), 256)
            gate = jnp.dot(xs[...], wg[src, :, cut], preferred_element_type=F32)
            up = jnp.dot(xs[...], wu[src, :, cut], preferred_element_type=F32)
            act[src, :, cut] = (gate / (1.0 + jnp.exp(-gate)) * up).astype(BF16)

    for c in locals_:
        c.wait()
    hidden_units(col)
    w_got(3, 1)
    w_relay(1, 1).start()
    w_got(2, 0)
    w_got(3, 0)
    hidden_units(xleft)
    hidden_units(xright)
    w_got(4, 0)
    w_relay(2, 0).start()
    w_got(5, 1)
    w_relay(2, 1).start()
    w_got(5, 0)
    w_got(4, 1)
    for way in range(2):
        for r in range(2):
            w_relay(r, way).wait_recv()
    hidden_units(lax.rem(col + 2, 4))
    for way in range(2):
        w_relay(2, way).wait_recv()

    def mate_part(n):
        return remote(pout.at[n], pin.at[n], px_s.at[n], px_r.at[n], mate)

    def own_part(n, zz):
        b = lax.rem(zz, 8)
        return part[n, tgt_ref[b * 2 + core]].astype(F32) + pin[n, b].astype(F32)

    def ring(n, s, way):
        src, dst, ss, rs, dev = (sr, rr, rr_s, rr_r, right) if way == 0 else (sl, rl, rl_s, rl_r, left)
        lo, cnt = (way * 64, 64) if s == 0 else (0, 128)
        cut = pl.ds(lo, cnt)
        return remote(src.at[n, s, cut], dst.at[n, s, cut], ss.at[n, s], rs.at[n, s], dev)

    def first(n):
        mate_part(n).wait_recv()
        far = own_part(n, z + 4).astype(BF16)
        sr[n, 0, pl.ds(0, 64)] = far[:64]
        sl[n, 0, pl.ds(64, 64)] = far[64:]
        ring(n, 0, 0).start()
        ring(n, 0, 1).start()

    @pl.loop(0, NCH)
    def _(n):
        cut = pl.ds(pl.multiple_of(n * CW, CW), CW)
        total = jnp.dot(act[0], wd[0, :, cut], preferred_element_type=F32)
        for src in range(1, 4):
            total = total + jnp.dot(act[src], wd[src, :, cut], preferred_element_type=F32)
        for k in range(4):
            part[n, k] = total[k * 128 : (k + 1) * 128].astype(BF16)
        part[n, 4] = jnp.zeros((128, CW), BF16)
        for zz in range(8):
            pout[n, zz] = part[n, tgt_ref[zz * 2 + 1 - core]]
        mate_part(n).start()

        @pl.when(n >= 1)
        def _():
            first(n - 1)

    first(NCH - 1)

    for s in range(1, 4):
        @pl.loop(0, NCH)
        def _(n):
            for way in range(2):
                ring(n, s - 1, way).wait_recv()
                here = own_part(n, z + 4 - s if way == 0 else z + 4 + s)
                buf, got = (sr, rr) if way == 0 else (sl, rl)
                if s == 1:
                    lo, other = way * 64, 64 - way * 64
                    buf[n, s, pl.ds(lo, 64)] = (
                        here[lo : lo + 64] + got[n, 0, pl.ds(lo, 64)].astype(F32)
                    ).astype(BF16)
                    buf[n, s, pl.ds(other, 64)] = here[other : other + 64].astype(BF16)
                else:
                    buf[n, s] = (here + got[n, s - 1].astype(F32)).astype(BF16)
                ring(n, s, way).start()

    def y_send(n):
        cut = pl.ds(pl.multiple_of(n * CW, CW), CW)
        return remote(yout.at[n], out_ref.at[:, cut], y_s.at[n], y_r.at[n], yn)

    @pl.loop(0, NCH)
    def _(n):
        for way in range(2):
            ring(n, 3, way).wait_recv()
        cut = pl.ds(pl.multiple_of(n * CW, CW), CW)
        ffn = (own_part(n, z) + rr[n, 3].astype(F32) + rl[n, 3].astype(F32)).astype(BF16)
        yout[n] = (hid[:, cut].astype(F32) + ffn.astype(F32)).astype(BF16)
        y_send(n).start()

    @pl.loop(1, 8)
    def _(k):
        j = lax.rem(i + k, 8)
        a2a_copy(j).wait_send()
        st_copy(j).wait_send()

    @pl.loop(grp + 1, 8)
    def _(g):
        tot_copy(g).wait_send()

    for way in range(2):
        for k in range(6):
            w_own(k, way).wait_send()
        for r in range(3):
            w_relay(r, way).wait_send()
        for s in range(4):
            for hv in range(2):
                if s < 3 or hv == way:
                    ag_send(s, hv, way).wait_send()
    for dz in range(8):
        for hv in range(2):
            mate_send(dz, hv).wait_send()

    @pl.loop(0, NCH)
    def _(n):
        mate_part(n).wait_send()
        for s in range(4):
            for way in range(2):
                ring(n, s, way).wait_send()
        y_send(n).wait()


def run_tick(sel, tgt, ab, qp, o0, x, og, wo, fg, gate, up, down):
    vmem = pl.BlockSpec(memory_space=pltpu.VMEM)
    smem = pl.BlockSpec(memory_space=pltpu.SMEM)
    hbm = pl.BlockSpec(memory_space=pl.ANY)
    V = pltpu.VMEM
    D = pltpu.SemaphoreType.DMA
    return pl.pallas_call(
        tick_kernel,
        out_shape=jax.ShapeDtypeStruct((128, 1024), BF16),
        in_specs=[smem, smem] + [vmem] * 7 + [hbm] * 3,
        out_specs=vmem,
        scratch_shapes=[
            V((8, 256, 128), BF16), V((9, 256, 128), F32), V((256, 128), BF16),
            V((8, 256, 128), BF16), V((8, 128, 128), BF16), V((8, 128, 128), BF16),
            V((128, 1024), BF16), V((128, 1024), BF16), V((16, 128, 1024), BF16),
            V((512, 1024), BF16), V((4, 1024, 512), BF16), V((4, 1024, 512), BF16),
            V((4, 512, 1024), BF16), V((4, 512, 512), BF16), V((NCH, 5, 128, CW), BF16),
            V((NCH, 8, 128, CW), BF16), V((NCH, 8, 128, CW), BF16),
            V((NCH, 4, 128, CW), BF16), V((NCH, 4, 128, CW), BF16),
            V((NCH, 4, 128, CW), BF16), V((NCH, 4, 128, CW), BF16), V((NCH, 128, CW), BF16),
            V((128, 128), F32),
            D((3,)), D((8,)), D((8,)), D((8,)), D((8,)), D((8,)), D((8,)),
            D((2, 9)), D((2, 9)), D((2, 8)), D((2, 8)), D((16,)), D((16,)),
            D((NCH,)), D((NCH,)), D((NCH, 4)), D((NCH, 4)), D((NCH, 4)), D((NCH, 4)),
            D((NCH,)), D((NCH,)),
        ],
        compiler_params=pltpu.CompilerParams(
            collective_id=0, has_side_effects=True, vmem_limit_bytes=60 * 1024 * 1024
        ),
        name="tick",
    )(sel, tgt, ab, qp, o0, x, og, wo, fg, gate, up, down)


def per_device(
    held, log_decay, route_ids, norm_gain, qkv_weight, beta_weight, out_gain, out_weight,
    ffn_gain, gate_weight, up_weight, down_weight,
):
    ein = partial(jnp.einsum, precision=lax.Precision.HIGHEST)
    x_rows = held[0]
    steps_dev, width = x_rows.shape
    heads = log_decay.shape[2]
    head_dim = width // heads
    xf = x_rows.astype(F32)
    xn = rms(xf, norm_gain[0]).astype(BF16)
    qkv = jnp.dot(xn, qkv_weight[0], preferred_element_type=F32).astype(BF16).astype(F32)
    qkv = qkv.reshape(steps_dev, 3, heads, head_dim).transpose(1, 2, 0, 3)
    q, k, v = qkv[0], qkv[1], qkv[2]
    q = q * lax.rsqrt(jnp.sum(q * q, axis=-1, keepdims=True) + 1e-06)
    k = k * lax.rsqrt(jnp.sum(k * k, axis=-1, keepdims=True) + 1e-06)
    beta = jax.nn.sigmoid(jnp.dot(xn, beta_weight[0], preferred_element_type=F32)).T
    cumul, w_part, u_part, trans_a, trans_b = span_terms(k, v, beta, log_decay[0].T)
    posit = jnp.arange(steps_dev)
    incl = posit[:, None] >= posit[None, :]
    differ = cumul[:, :, None] - cumul[:, None, :]
    ratio = jnp.where(incl, jnp.exp(jnp.where(incl, differ, 0.0)), 0.0)
    scores = ein("htd,hsd->hts", q, k) * ratio
    qp = jnp.exp(cumul)[:, :, None] * q - ein("hts,hsk->htk", scores, w_part)
    o0 = ein("hts,hsv->htv", scores, u_part)
    ab = jnp.concatenate([trans_a, trans_b], axis=1).astype(BF16)

    place = lax.axis_index("seq")
    kinds = lax.dynamic_slice_in_dim(route_ids[0, :, 0], place // 16 * 16, 16)
    index = jnp.arange(16)
    same = (kinds[:, None] == kinds[None, :]) & (index[:, None] // 8 == index[None, :] // 8)
    rank = jnp.sum((same & (index[None, :] < index[:, None])).astype(jnp.int32), axis=1)
    mine = kinds == place % EXPERTS
    tgt = jnp.where(mine, index // 8 * 2 + rank, 4).astype(jnp.int32)
    slots = jnp.arange(4)
    sel = jnp.sum(jnp.where(tgt[None, :] == slots[:, None], index[None, :], 0), axis=1).astype(
        jnp.int32
    )
    out = run_tick(
        sel, tgt, ab, qp, o0, x_rows, out_gain, out_weight[0], ffn_gain,
        gate_weight[0, 0], up_weight[0, 0], down_weight[0, 0],
    )
    return out[None]


def solution(mesh):
    placed = (
        P("segment", "seq", None),
        P("segment", "seq", None),
        P("segment", None, None),
        P("segment", None),
        P("segment", None, None),
        P("segment", None, None),
        P("segment", None),
        P("segment", None, None),
        P("segment", None),
        P("segment", "seq", None, None),
        P("segment", "seq", None, None),
        P("segment", "seq", None, None),
    )
    return jax.shard_map(
        per_device, mesh=mesh, in_specs=placed, out_specs=P("segment", "seq", None), check_vma=False
    )
```

time: 860 us -> 198 us (0.23); the launches traced: 847 us -> 198 us
  waiting for transfers between devices: 551 us -> 0 us
  Pallas kernels: 0 us -> 169 us
  starting transfers between devices: 163 us -> 0 us
  matrix products: 58.1 us -> 21.4 us
  other arithmetic: 37.3 us -> 3.99 us
  local copies, waits for them, and re-layouts: 21.7 us -> 3.06 us
  between operations: 15.4 us -> 0.27 us
    ppermute x13 -> x0, waiting for transfers between devices: 360 us -> none  [the longest x12 352 us: swapped(): return lax.ppermute(block, axis, route)]
    all_gather x2 -> x0, waiting for transfers between devices: 191 us -> none  [carried_in(): lax.all_gather(a.astype(kind), axis)]
    pallas_call x0 -> x1, Pallas kernels: none -> 169 us  [run_tick(): pl.pallas_call(tick_kernel, out_shape=jax.ShapeDtypeStruct((128, 1024), B...]
    ppermute x13 -> x0, starting transfers between devices: 163 us -> none  [the longest x12 162 us: swapped(): return lax.ppermute(block, axis, route)]
    dot_general x17 -> x5, matrix products: 42.8 us -> 8.55 us  [the longest x1 3.95 us: per_device(): jnp.dot(xn, qkv_weight[0], preferred_element_type=F32).astype(BF16)]
    select_n x10 -> x2, other arithmetic: 22.2 us -> 0.08 us  [per_device(): tgt = jnp.where(mine, index // 8 * 2 + rank, 4).astype(jnp.int32)]
    unnamed x36 -> x13, local copies, waits for them, and re-layouts: 10.4 us -> 1.7 us
  transfers between devices with their start and end apart: 15 -> 0, of which waited for: 15 -> 0; matrix products, arithmetic and copies ran while one was open for 2% -> 0% of each run, Pallas kernels for 0% -> 0%
where the time goes in v1:
time: 198 us
  Pallas kernels  169 us (85%)
  matrix products  21.4 us (11%)
  other arithmetic  3.99 us (2%)
  local copies, waits for them, and re-layouts  3.06 us (2%)
    pallas_call x1, Pallas kernels, run_tick(): pl.pallas_call(tick_kernel, out_shape=jax.ShapeDtypeStruct((128, 1024), B...  169 us

profile of v1, /device:TPU:96, one launch (start us, length us, event | category | flops | bytes accessed | tf_op | source)
XLA Modules:
  0.0 197.6 jit_solution(6431434496496936019)
XLA Ops:
  0.0 1.1 multiply_reduce_fusion.2
  1.1 3.9 %fusion.5 = f32[128,3072]{1,0:T(8,128)S(1)} fusion(bf16[1,1024,3072]{2,1,0:T(8,128)(2,1)} %param.16, bf16[1,128,1024]{2,1,0:T(8,128)(2,1)} %param.12, f32[1024]{0:T(1024)} %bitcast.106, f32[128]{0:T(128)S(1)} %add_rsqrt_fusion.2), kind=kOutput, calls=%fused_computation.3 | convolution fusion | flops 806617088 | bytes 8131072 | tf_op jit(solution)/shard_map/dot_general | solution.py:469
  7.2 1.4 fusion.8
  8.6 0.6 fusion.56
  9.2 0.7 convolution_add_fusion.5
  9.9 0.6 fusion.57
  10.5 0.6 convolution_add_fusion.4
  11.8 0.6 convolution_add_fusion.3
  12.5 0.6 fusion.59
  13.1 0.6 convolution_add_fusion.2
  13.7 0.6 fusion.60
  14.4 0.6 convolution_add_fusion.1
  15.0 0.6 fusion.61
  15.7 0.6 convolution_add_fusion
  16.8 1.2 fusion.14
  18.0 1.3 convolution_multiply_fusion
  19.4 1.5 fusion.27.o0_ref
  20.9 1.5 convolution_subtract_fusion.qp_ref
  22.6 1.3 fusion.9
  23.9 1.3 convolution_convert_fusion
  25.2 0.8 pad_maximum_fusion.ab_ref
  26.4 0.6 select_reduce_fusion.sel_ref
  27.0 169.0 %tick.1 = bf16[128,1024]{1,0:T(8,128)(2,1)} custom-call(s32[4]{0:T(128)} %select_reduce_fusion.sel_ref, s32[16]{0:T(128)} %copy-done.4, bf16[8,256,128]{2,1,0:T(8,128)(2,1)} %pad_maximum_fusion.ab_ref, f32[8,128,128]{2,1,0:T(8,128)} %convolution_subtract_fusion.qp_ref, f32[8,128,128]{2,1,0:T(8,128)} %fusion.27.o0_ref, bf16[128,1024]{1,0:T(8,128)(2,1)} %bitcast.100, ...), custom_call_target="tpu_custom_call" | custom-call | tf_op jit(solution)/shard_map/tick/pallas_call | solution.py:431
  196.0 1.7 copy.26
  (30 shorter events, 3.7 us)
Async XLA Ops:
  0.0 6.9 %copy-start = (bf16[1,1024,8]{1,2,0:T(8,128)(2,1)S(1)}, bf16[1,1024,8]{1,2,0:T(8,128)(2,1)}, u32[]{:S(2)}) copy-start(bf16[1,1024,8]{1,2,0:T(8,128)(2,1)} %param.17) | copy-start | bytes 49156
  5.5 0.9 copy-start.3
  5.5 1.3 copy-start.1
  5.6 1.3 copy-start.2
  22.6 3.4 %copy-start.5 = (s32[1,64,1]{1,2,0:T(1,128)S(1)}, s32[1,64,1]{1,2,0:T(1,128)}, u32[]{:S(2)}) copy-start(s32[1,64,1]{1,2,0:T(1,128)} %param.14) | copy-start | bytes 772
  26.4 0.6 copy-start.4

commit v2 on v1

--- a/solution.py
+++ b/solution.py
@@ -1,5 +1,3 @@
-from functools import partial
-
 import jax
 import jax.numpy as jnp
 from jax import lax
@@ -10,49 +8,7 @@
 EXPERTS = 8
 
 
-def rms(values, gain):
-    return values * lax.rsqrt(jnp.mean(values * values, axis=-1, keepdims=True) + 1e-06) * gain
-
-
-def unit_lower_solve(strict_part, rhs):
-    ein = partial(jnp.einsum, precision=lax.Precision.HIGHEST)
-    length = strict_part.shape[-1]
-    raised = -strict_part
-    running = jnp.eye(length, dtype=jnp.float32) + raised
-    for _ in range((length - 1).bit_length() - 1):
-        raised = ein("hij,hjk->hik", raised, raised)
-        running = running + ein("hij,hjk->hik", running, raised)
-    return ein("hij,hjk->hik", running, rhs)
-
-
-def span_terms(lookup_vectors, values, beta, logd):
-    ein = partial(jnp.einsum, precision=lax.Precision.HIGHEST)
-    length = lookup_vectors.shape[1]
-    dim_k = lookup_vectors.shape[2]
-    cumul = jnp.cumsum(logd, axis=-1)
-    posit = jnp.arange(length)
-    strict = posit[:, None] > posit[None, :]
-    differ = cumul[:, :, None] - cumul[:, None, :]
-    ratio = jnp.where(strict, jnp.exp(jnp.where(strict, differ, 0.0)), 0.0)
-    inner = ein("htd,hsd->hts", lookup_vectors, lookup_vectors)
-    strict_part = beta[:, :, None] * ratio * inner
-    growth = jnp.exp(cumul)
-    rhs = jnp.concatenate(
-        [(beta * growth)[:, :, None] * lookup_vectors, beta[:, :, None] * values], axis=-1
-    )
-    solved = unit_lower_solve(strict_part, rhs)
-    w_part = solved[..., :dim_k]
-    u_part = solved[..., dim_k:]
-    tail = jnp.exp(cumul[:, -1:] - cumul)
-    scaled = tail[:, :, None] * lookup_vectors
-    trans_a = growth[:, -1][:, None, None] * jnp.eye(dim_k, dtype=jnp.float32) - ein(
-        "hck,hcj->hkj", w_part, scaled
-    )
-    trans_b = ein("hcv,hck->hvk", u_part, scaled)
-    return (cumul, w_part, u_part, trans_a, trans_b)
-
-
-LEG = ("segment", "seq")
+HU = 4
 MESH = pl.DeviceIdType.MESH
 NCH = 4
 CW = 256
@@ -64,13 +20,21 @@
     return jnp.dot(a, b, precision=lax.Precision.HIGHEST, preferred_element_type=F32)
 
 
+def split_dot(a, b):
+    high = a.astype(BF16)
+    low = (a - high.astype(F32)).astype(BF16)
+    return jnp.dot(high, b, preferred_element_type=F32) + jnp.dot(
+        low, b, preferred_element_type=F32
+    )
+
+
 def tick_kernel(
-    sel_ref, tgt_ref, ab_ref, qp_ref, o0_ref, x_ref, og_ref, wo_ref, fg_ref,
-    gate_hbm, up_hbm, down_hbm,
+    sel_ref, tgt_ref, x_ref, logd_ref, ng_ref, bw_ref, og_ref, fg_ref,
+    wq_hbm, wo_hbm, gate_hbm, up_hbm, down_hbm,
     out_ref,
-    ab_in, tp, tot_out, tot_in, s_out, s_in, on, hid, gath, xs, wg, wu, wd, act, part,
+    wq, wo_ref, qkv, lb, bb, eg, et, qp_ref, o0_ref, ab_ref, ab_in, tp, tot_out, tot_in, s_out, s_in, on, hid, gath, xs, wg, wu, wd, act, part,
     pout, pin, sr, sl, rr, rl, yout, entering,
-    lsem, a2a_s, a2a_r, tot_s, tot_r, st_s, st_r, w_s, w_r, ag_s, ag_r, pf_s, pf_r,
+    lsem, qsem, a2a_s, a2a_r, tot_s, tot_r, st_s, st_r, w_s, w_r, ag_s, ag_r, pf_s, pf_r,
     px_s, px_r, rr_s, rr_r, rl_s, rl_r, y_s, y_r,
 ):
     seg = lax.axis_index("segment")
@@ -98,6 +62,15 @@
     yn = (lax.rem(seg + 1, 4), me)
     yp = (lax.rem(seg + 3, 4), me)
 
+    fetches = [
+        pltpu.make_async_copy(
+            wq_hbm.at[:, pl.ds(n * 512, 512)], wq.at[:, pl.ds(n * 512, 512)], qsem.at[n]
+        )
+        for n in range(6)
+    ] + [pltpu.make_async_copy(wo_hbm, wo_ref, qsem.at[6])]
+    for c in fetches:
+        c.start()
+
     barrier = pltpu.get_barrier_semaphore()
     for k in range(1, 8):
         pl.semaphore_signal(barrier, inc=1, device_id=(seg, grp * 8 + lax.rem(i + k, 8)), device_id_type=MESH)
@@ -111,10 +84,6 @@
 
     def a2a_from(j):
         return remote(ab_ref.at[j], ab_in.at[j], a2a_s.at[j], a2a_r.at[j], (seg, grp * 8 + j))
-
-    @pl.loop(1, 8)
-    def _(k):
-        a2a_copy(lax.rem(i + k, 8)).start()
 
     xleft, xright = lax.rem(col + 3, 4), lax.rem(col + 1, 4)
     hbms = (gate_hbm, up_hbm, down_hbm)
@@ -145,11 +114,90 @@
     def w_got(k, way):
         w_own(k, way).wait_recv()
 
-    w_own(0, 0).start()
-    w_own(0, 1).start()
+    for k in range(3):
+        w_own(k, 0).start()
+        w_own(k, 1).start()
     locals_ = [pltpu.make_async_copy(hbms[a], bufs[a].at[col], lsem.at[a]) for a in range(3)]
     for c in locals_:
         c.start()
+
+    xf = x_ref[...].astype(F32)
+    xn = (
+        xf * lax.rsqrt(jnp.mean(xf * xf, axis=-1, keepdims=True) + 1e-06) * ng_ref[...]
+    ).astype(BF16)
+    for n in range(6):
+        fetches[n].wait()
+        cut = pl.ds(n * 512, 512)
+        qkv[:, cut] = jnp.dot(xn, wq[:, cut], preferred_element_type=F32).astype(BF16)
+    beta = jnp.dot(xn, bw_ref[...], preferred_element_type=F32)
+    beta = 1.0 / (1.0 + jnp.exp(-beta))
+    r128 = lax.broadcasted_iota(jnp.int32, (128, 128), 0)
+    c128 = lax.broadcasted_iota(jnp.int32, (128, 128), 1)
+    incl = jnp.where(r128 >= c128, 1.0, 0.0).astype(F32)
+    upper = jnp.where(r128 < c128, 1.0, 0.0).astype(F32)
+    eye = jnp.where(r128 == c128, 1.0, 0.0).astype(F32)
+    logd = logd_ref[...]
+    growth = jnp.exp(hdot(incl, logd))
+    tail = jnp.exp(hdot(upper, logd))
+    for h in range(8):
+        lb[h] = jnp.broadcast_to(logd[:, h : h + 1], (128, 128))
+        bb[h] = jnp.broadcast_to(beta[:, h : h + 1], (128, 128))
+        eg[h] = jnp.broadcast_to(growth[:, h : h + 1], (128, 128))
+        et[h] = jnp.broadcast_to(tail[:, h : h + 1], (128, 128))
+
+    def norm(v):
+        return v * lax.rsqrt(jnp.sum(v * v, axis=-1, keepdims=True) + 1e-06)
+
+    def across(a, b):
+        return lax.dot_general(
+            a, b, (((1,), (1,)), ((), ())),
+            precision=lax.Precision.HIGHEST, preferred_element_type=F32,
+        )
+
+    def head_part(h, base):
+        cut = pl.ds(pl.multiple_of(base + h * 128, 128), 128)
+        return qkv[:, cut].astype(F32)
+
+    @pl.loop(0, 8 // HU)
+    def _(it):
+        hs = [it * HU + u for u in range(HU)]
+        qs = [norm(head_part(h, 0)) for h in hs]
+        ks = [norm(head_part(h, 1024)) for h in hs]
+        ratio = [
+            jnp.where(r128 >= c128, jnp.exp(hdot(incl, jnp.where(r128 > c128, lb[h], 0.0))), 0.0)
+            for h in hs
+        ]
+        both = [across(jnp.concatenate([k, q], axis=0), k) for k, q in zip(ks, qs)]
+        raised = [
+            -jnp.where(r128 > c128, bb[h] * ra * bo[:128], 0.0)
+            for h, ra, bo in zip(hs, ratio, both)
+        ]
+        scores = [bo[128:] * ra for bo, ra in zip(both, ratio)]
+        running = [eye + r for r in raised]
+        for _ in range(6):
+            raised = [hdot(r, r) for r in raised]
+            running = [w + hdot(w, r) for w, r in zip(running, raised)]
+        solved = [
+            hdot(
+                w,
+                jnp.concatenate(
+                    [bb[h] * eg[h] * k, bb[h] * head_part(h, 2048)], axis=1
+                ),
+            )
+            for h, w, k in zip(hs, running, ks)
+        ]
+        moved = [hdot(jnp.transpose(so), et[h] * k) for h, so, k in zip(hs, solved, ks)]
+        outs = [hdot(sc, so) for sc, so in zip(scores, solved)]
+        for h, q, mo, ou in zip(hs, qs, moved, outs):
+            last = eg[h, 127:128, :]
+            ab_ref[h, :128, :] = (last * eye - mo[:128]).astype(BF16)
+            ab_ref[h, 128:, :] = mo[128:].astype(BF16)
+            qp_ref[h] = eg[h] * q - ou[:, :128]
+            o0_ref[h] = ou[:, 128:]
+
+            @pl.when(h != i)
+            def _():
+                a2a_copy(h).start()
 
     ab_in[i] = ab_ref[i]
 
@@ -168,8 +216,8 @@
         def _():
             a2a_from(j).wait_recv()
 
-        low = ab_in[j].astype(F32)
-        tp[j + 1] = hdot(tp[j], low[:128]) + jnp.where(rows >= 128, low, 0.0)
+        low = ab_in[j]
+        tp[j + 1] = split_dot(tp[j], low[:128]) + jnp.where(rows >= 128, low.astype(F32), 0.0)
 
     tot_out[...] = tp[8].astype(BF16)
 
@@ -183,13 +231,17 @@
     def _(g):
         tot_copy(g).start()
 
+    for k in range(3, 6):
+        w_own(k, 0).start()
+        w_own(k, 1).start()
+
     entering[...] = jnp.zeros((128, 128), F32)
 
     @pl.loop(0, grp)
     def _(g):
         tot_from(g).wait_recv()
-        pair = tot_in[g].astype(F32)
-        entering[...] = hdot(entering[...], pair[:128]) + pair[128:]
+        pair = tot_in[g]
+        entering[...] = split_dot(entering[...], pair[:128]) + pair[128:].astype(F32)
 
     def st_copy(j):
         return remote(s_out.at[j], s_in.at[i], st_s.at[j], st_r.at[i], (seg, grp * 8 + j))
@@ -197,39 +249,44 @@
     def st_from(j):
         return remote(s_out.at[j], s_in.at[j], st_s.at[j], st_r.at[j], (seg, grp * 8 + j))
 
-    @pl.loop(0, 8)
-    def _(j):
+    state = entering[...]
+    for j in range(8):
         pre = tp[j]
-        entered = (hdot(entering[...], pre[:128]) + pre[128:]).astype(BF16)
-        s_out[j] = entered
-
-        @pl.when(j == i)
-        def _():
-            s_in[j] = entered
+        s_out[j] = (hdot(state, pre[:128]) + pre[128:]).astype(BF16)
 
         @pl.when(j != i)
         def _():
             st_copy(j).start()
 
-    for k in range(1, 6):
-        w_own(k, 0).start()
-        w_own(k, 1).start()
+    s_in[i] = s_out[i]
+
     w_got(0, 0)
     w_relay(0, 0).start()
     w_got(0, 1)
-
-    @pl.loop(0, 8)
-    def _(h):
+    w_got(1, 0)
+    w_relay(1, 0).start()
+    w_got(1, 1)
+    w_got(2, 0)
+    w_got(2, 1)
+    w_relay(0, 1).start()
+
+    for h in range(8):
         @pl.when(h != i)
         def _():
             st_from(h).wait_recv()
 
-        o = o0_ref[h] + lax.dot_general(
-            qp_ref[h], s_in[h].astype(F32), (((1,), (1,)), ((), ())),
-            precision=lax.Precision.HIGHEST, preferred_element_type=F32,
+    fetches[6].wait()
+    for h in range(8):
+        qp = qp_ref[h]
+        high = qp.astype(BF16)
+        low = (qp - high.astype(F32)).astype(BF16)
+        dims = (((1,), (1,)), ((), ()))
+        o = o0_ref[h] + (
+            lax.dot_general(high, s_in[h], dims, preferred_element_type=F32)
+            + lax.dot_general(low, s_in[h], dims, preferred_element_type=F32)
         )
         o = o * lax.rsqrt(jnp.mean(o * o, axis=-1, keepdims=True) + 1e-06) * og_ref[...]
-        on[:, pl.ds(pl.multiple_of(h * 128, 128), 128)] = o.astype(BF16)
+        on[:, h * 128 : (h + 1) * 128] = o.astype(BF16)
 
     hidden = (
         x_ref[...].astype(F32) + jnp.dot(on[...], wo_ref[...], preferred_element_type=F32)
@@ -267,18 +324,20 @@
             ag_send(0, hv, way).start()
     for hv in range(2):
         mate_send(0, hv).start()
+    w_got(3, 1)
+    w_relay(1, 1).start()
     for s in range(1, 4):
+        if s == 3:
+            w_got(4, 0)
+            w_relay(2, 0).start()
+            w_got(5, 1)
+            w_relay(2, 1).start()
         for hv in range(2):
             for way in range(2):
                 ag_recv(s - 1, hv, way).wait_recv()
                 if s < 3 or hv == way:
                     ag_send(s, hv, way).start()
                 mate_send(8 - s if way == 0 else s, hv).start()
-    w_got(1, 0)
-    w_relay(1, 0).start()
-    w_got(1, 1)
-    w_got(2, 1)
-    w_relay(0, 1).start()
     ag_recv(3, 0, 0).wait_recv()
     mate_send(4, 0).start()
     ag_recv(3, 1, 1).wait_recv()
@@ -301,16 +360,9 @@
     for c in locals_:
         c.wait()
     hidden_units(col)
-    w_got(3, 1)
-    w_relay(1, 1).start()
-    w_got(2, 0)
     w_got(3, 0)
     hidden_units(xleft)
     hidden_units(xright)
-    w_got(4, 0)
-    w_relay(2, 0).start()
-    w_got(5, 1)
-    w_relay(2, 1).start()
     w_got(5, 0)
     w_got(4, 1)
     for way in range(2):
@@ -422,7 +474,7 @@
         y_send(n).wait()
 
 
-def run_tick(sel, tgt, ab, qp, o0, x, og, wo, fg, gate, up, down):
+def run_tick(sel, tgt, x, logd, ng, bw, og, fg, wq, wo, gate, up, down):
     vmem = pl.BlockSpec(memory_space=pltpu.VMEM)
     smem = pl.BlockSpec(memory_space=pltpu.SMEM)
     hbm = pl.BlockSpec(memory_space=pl.ANY)
@@ -431,9 +483,13 @@
     return pl.pallas_call(
         tick_kernel,
         out_shape=jax.ShapeDtypeStruct((128, 1024), BF16),
-        in_specs=[smem, smem] + [vmem] * 7 + [hbm] * 3,
+        in_specs=[smem, smem] + [vmem] * 6 + [hbm] * 5,
         out_specs=vmem,
         scratch_shapes=[
+            V((1024, 3072), BF16), V((1024, 1024), BF16), V((128, 3072), BF16),
+            V((8, 128, 128), F32), V((8, 128, 128), F32), V((8, 128, 128), F32),
+            V((8, 128, 128), F32), V((8, 128, 128), F32), V((8, 128, 128), F32),
+            V((8, 256, 128), BF16),
             V((8, 256, 128), BF16), V((9, 256, 128), F32), V((256, 128), BF16),
             V((8, 256, 128), BF16), V((8, 128, 128), BF16), V((8, 128, 128), BF16),
             V((128, 1024), BF16), V((128, 1024), BF16), V((16, 128, 1024), BF16),
@@ -443,7 +499,7 @@
             V((NCH, 4, 128, CW), BF16), V((NCH, 4, 128, CW), BF16),
             V((NCH, 4, 128, CW), BF16), V((NCH, 4, 128, CW), BF16), V((NCH, 128, CW), BF16),
             V((128, 128), F32),
-            D((3,)), D((8,)), D((8,)), D((8,)), D((8,)), D((8,)), D((8,)),
+            D((3,)), D((7,)), D((8,)), D((8,)), D((8,)), D((8,)), D((8,)), D((8,)),
             D((2, 9)), D((2, 9)), D((2, 8)), D((2, 8)), D((16,)), D((16,)),
             D((NCH,)), D((NCH,)), D((NCH, 4)), D((NCH, 4)), D((NCH, 4)), D((NCH, 4)),
             D((NCH,)), D((NCH,)),
@@ -452,36 +508,13 @@
             collective_id=0, has_side_effects=True, vmem_limit_bytes=60 * 1024 * 1024
         ),
         name="tick",
-    )(sel, tgt, ab, qp, o0, x, og, wo, fg, gate, up, down)
+    )(sel, tgt, x, logd, ng, bw, og, fg, wq, wo, gate, up, down)
 
 
 def per_device(
     held, log_decay, route_ids, norm_gain, qkv_weight, beta_weight, out_gain, out_weight,
     ffn_gain, gate_weight, up_weight, down_weight,
 ):
-    ein = partial(jnp.einsum, precision=lax.Precision.HIGHEST)
-    x_rows = held[0]
-    steps_dev, width = x_rows.shape
-    heads = log_decay.shape[2]
-    head_dim = width // heads
-    xf = x_rows.astype(F32)
-    xn = rms(xf, norm_gain[0]).astype(BF16)
-    qkv = jnp.dot(xn, qkv_weight[0], preferred_element_type=F32).astype(BF16).astype(F32)
-    qkv = qkv.reshape(steps_dev, 3, heads, head_dim).transpose(1, 2, 0, 3)
-    q, k, v = qkv[0], qkv[1], qkv[2]
-    q = q * lax.rsqrt(jnp.sum(q * q, axis=-1, keepdims=True) + 1e-06)
-    k = k * lax.rsqrt(jnp.sum(k * k, axis=-1, keepdims=True) + 1e-06)
-    beta = jax.nn.sigmoid(jnp.dot(xn, beta_weight[0], preferred_element_type=F32)).T
-    cumul, w_part, u_part, trans_a, trans_b = span_terms(k, v, beta, log_decay[0].T)
-    posit = jnp.arange(steps_dev)
-    incl = posit[:, None] >= posit[None, :]
-    differ = cumul[:, :, None] - cumul[:, None, :]
-    ratio = jnp.where(incl, jnp.exp(jnp.where(incl, differ, 0.0)), 0.0)
-    scores = ein("htd,hsd->hts", q, k) * ratio
-    qp = jnp.exp(cumul)[:, :, None] * q - ein("hts,hsk->htk", scores, w_part)
-    o0 = ein("hts,hsv->htv", scores, u_part)
-    ab = jnp.concatenate([trans_a, trans_b], axis=1).astype(BF16)
-
     place = lax.axis_index("seq")
     kinds = lax.dynamic_slice_in_dim(route_ids[0, :, 0], place // 16 * 16, 16)
     index = jnp.arange(16)
@@ -494,8 +527,8 @@
         jnp.int32
     )
     out = run_tick(
-        sel, tgt, ab, qp, o0, x_rows, out_gain, out_weight[0], ffn_gain,
-        gate_weight[0, 0], up_weight[0, 0], down_weight[0, 0],
+        sel, tgt, held[0], log_decay[0], norm_gain, beta_weight[0], out_gain, ffn_gain,
+        qkv_weight[0], out_weight[0], gate_weight[0, 0], up_weight[0, 0], down_weight[0, 0],
     )
     return out[None]
 

time: 198 us -> 161 us (0.81)
  the two profiles are of different devices: /device:TPU:96 before, /device:TPU:67 now
where the time goes in v2:
time: 161 us
  Pallas kernels  154 us (96%)
  local copies, waits for them, and re-layouts  5.36 us (3%)
  other arithmetic  1.62 us (1%)
    pallas_call x1, Pallas kernels, run_tick(): pl.pallas_call(tick_kernel, out_shape=jax.ShapeDtypeStruct((128, 1024), B...  154 us
    unnamed x5, local copies, waits for them, and re-layouts  4.63 us

profile of v2, /device:TPU:67, one launch (start us, length us, event | category | flops | bytes accessed | tf_op | source)
XLA Modules:
  0.0 160.6 jit_solution(333987098175530522)
XLA Ops:
  0.0 0.7 dynamic-slice_bitcast_fusion
  0.7 0.2 convert_reduce_fusion
  0.9 0.7 compare_select_fusion.tgt_ref
  1.6 0.0 copy-start
  1.6 0.7 select_reduce_fusion.sel_ref
  2.4 1.4 copy.15
  3.8 1.6 copy.16
  5.3 0.0 copy-done
  5.3 153.6 %tick.1 = bf16[128,1024]{1,0:T(8,128)(2,1)} custom-call(s32[4]{0:T(128)} %select_reduce_fusion.sel_ref, s32[16]{0:T(128)} %copy-done, bf16[128,1024]{1,0:T(8,128)(2,1)} %bitcast.21, f32[128,8]{1,0:T(8,128)} %bitcast.20, f32[1,1024]{1,0:T(1,128)} %ng_ref.1, bf16[1024,8]{1,0:T(8,128)(2,1)} %bitcast.19, f32[1,128]{1,0:T(1,128)} %og_ref.1, f32[1,1024]{1,0:T(1,128)} %fg_ref.1, ...), custom_call_target="tpu_custom_call" | custom-call | tf_op jit(solution)/shard_map/tick/pallas_call | solution.py:483
  158.9 1.7 %copy.18 = bf16[1,128,1024]{2,1,0:T(8,128)(2,1)} copy(bf16[1,128,1024]{2,1,0:T(8,128)(2,1)} %bitcast.18) | data formatting | bytes 524288
  (1 shorter events, 0.0 us)
Async XLA Ops:
  1.6 3.7 %copy-start = (s32[16]{0:T(128)}, s32[16]{0:T(128)S(1)}, u32[]{:S(2)}) copy-start(s32[16]{0:T(128)S(1)} %compare_select_fusion.tgt_ref) | copy-start | bytes 196
